TPU v7x, 256 devices: a whole 4x4x8 slice. The times are simulated.
256 devices in a mesh: lon: 16 (over y, x), lat: 8 (over z), mem: 2 (over core).
Axes of the slice: x: 4, y: 4, z: 8, core: 2. Of those that a mesh axis runs over, the one named last changes fastest.
Arguments:
- anomalies: bfloat16 [128, 128, 4096], P('mem', 'lat', 'lon'), may hold values from -6 to 6
- state_mean: float32 [128, 4096], P('lat', 'lon'), may hold values from -6 to 6
- delayed_deviation_pair: bfloat16 [2, 128, 128, 4096], P(None, 'mem', 'lat', 'lon'), may hold values from -6 to 6
- lagged_means: float32 [2, 128, 4096], P(None, 'lat', 'lon'), may hold values from -6 to 6
- courant_lon: float32 [128, 4096], P('lat', 'lon'), may hold values from -0.45 to 0.45
- courant_lat: float32 [128, 4096], P('lat', 'lon'), may hold values from -0.45 to 0.45
- ocean: int32 [128, 4096], P('lat', 'lon'), may hold values 0 or 1
- obs_values: float32 [16384, 64], P(('lon', 'lat')), may hold values from -160 to 160
- obs_variance: float32 [16384, 64], P(('lon', 'lat')), may hold values from 2048 to 32768
- obs_cells: int32 [16384, 64], P(('lon', 'lat')), may hold values from 0 to 4095
- obs_tile: int32 [16384, 1], P(('lon', 'lat')), may hold values from 0 to 127; in each aligned block of 128 rows (0 to 127, 128 to 255, ...) at most 2 rows name the same one
- obs_count: int32 [16384], P(('lon', 'lat')), may hold values from 48 to 64
Outputs:
- analysis_anomalies: bfloat16 [3, 128, 128, 4096], P(None, 'mem', 'lat', 'lon')
- analysis_mean: float32 [3, 128, 4096], P(None, 'lat', 'lon')
Inputs may be any that keep to these rules, and one draw needn't show every extreme that they name: `obs_tile`: among the 128 blocks of one tile (an aligned run of rows) no tile is named more than 2 times.
All inputs are finite; a program needn't handle non-finite values. Where the computation divides by a largest or mean magnitude, that divisor is 1e-20 or more. No bound on the sum of `ocean` on one device may be relied on, other than what follows from the above.
Results may differ from a plain program's by a relative error of at most 0.0034.
Values may be sent and summed in bfloat16 or wider, within the bound.
A program may use at most 64 MiB of HBM per device.

v0:
```python
import math
import jax
import jax.numpy as jnp
from jax import lax
from jax.sharding import Mesh
from jax.sharding import PartitionSpec as P

SUBSTEPS = 4
NS_ITERS = 8
LON = ("lon_0", "lon_1")
LON_LAT = ("lon_0", "lon_1", "lat")


def with_halo(x, sides, width, wrap):
    for axis, dim in sides:
        count, length = (lax.axis_size(axis), x.shape[dim])
        up = [(i, (i + 1) % count) for i in range(count if wrap else count - 1)]
        down = [(j, i) for i, j in up]
        last = lax.slice_in_dim(x, length - width, length, axis=dim)
        leading = lax.slice_in_dim(x, 0, width, axis=dim)
        before = lax.ppermute(last, axis, up)
        after = lax.ppermute(leading, axis, down)
        x = jnp.concatenate([before, x, after], axis=dim)
    return x


def sent_together(arrays, axis, split_dim, concat_dim, along):
    widths = [a.shape[along] for a in arrays]
    both = jnp.concatenate(arrays, axis=along)
    out = lax.all_to_all(both, axis, split_axis=split_dim, concat_axis=concat_dim, tiled=True)
    return tuple(jnp.split(out, [sum(widths[:k]) for k in range(1, len(widths))], axis=along))


def over_axes(x, axes):
    for axis in axes:
        x = lax.psum(x, axis)
    return x


def side_by_side(arrays, axis, dim, along):
    widths = [math.prod(a.shape[along:]) for a in arrays]
    both = jnp.concatenate(
        [a.reshape(*a.shape[:along], w) for a, w in zip(arrays, widths)], axis=along
    )
    out = lax.all_gather(both, axis, axis=dim, tiled=True)
    blocks = jnp.split(out, [sum(widths[:k]) for k in range(1, len(widths))], axis=along)
    return tuple((b.reshape(*out.shape[:along], *a.shape[along:]) for a, b in zip(arrays, blocks)))


def upwind(center, western, eastern, southern, northern, courant_x, courant_y, wet_mask):
    tendency = (
        jnp.maximum(courant_x, 0.0) * (center - western)
        + jnp.minimum(courant_x, 0.0) * (eastern - center)
        + jnp.maximum(courant_y, 0.0) * (center - southern)
        + jnp.minimum(courant_y, 0.0) * (northern - center)
    )
    return center - wet_mask * tendency


def inverse_root(gram, projection):
    members = gram.shape[0]
    identity = jnp.eye(members, dtype=jnp.float32)
    system = (members - 1.0) * identity + 0.5 * (gram + gram.T)
    bound = jnp.max(jnp.sum(jnp.abs(system), axis=1))
    iterate = system / bound
    accum = identity
    for sweep in range(NS_ITERS):
        factor = 1.5 * identity - 0.5 * jnp.dot(accum, iterate, precision=lax.Precision.HIGHEST)
        iterate = jnp.dot(iterate, factor, precision=lax.Precision.HIGHEST)
        accum = jnp.dot(factor, accum, precision=lax.Precision.HIGHEST)
    root = accum / jnp.sqrt(bound)
    weights = jnp.dot(
        root,
        jnp.dot(root, projection, precision=lax.Precision.HIGHEST),
        precision=lax.Precision.HIGHEST,
    )
    transform = jnp.sqrt(members - 1.0) * root
    return (transform.astype(jnp.bfloat16), weights.astype(jnp.bfloat16))


def body(
    anomalies,
    state_mean,
    delayed_deviation_pair,
    lagged_means,
    courant_lon,
    courant_lat,
    ocean,
    obs_values,
    obs_variance,
    obs_cells,
    obs_tile,
    obs_count,
):
    locally_held_samples = anomalies.shape[0]
    wet_mask = ocean.astype(jnp.float32)
    coefficients = jnp.stack([courant_lon, courant_lat, wet_mask])
    sample_surfaces = jnp.concatenate([anomalies.astype(jnp.float32), state_mean[None]], 0)
    stacked = jnp.concatenate([sample_surfaces, coefficients], 0)
    widened = with_halo(stacked, ((LON, 2),), SUBSTEPS, True)
    extended = with_halo(widened.astype(jnp.bfloat16), (("lat", 1),), SUBSTEPS, False).astype(
        widened.dtype
    )
    field_count = sample_surfaces.shape[0]
    sample_surfaces = extended[:field_count]
    beside_all = extended[field_count:]
    for substep in range(SUBSTEPS):
        inner = beside_all[
            :,
            substep + 1 : beside_all.shape[1] - substep - 1,
            substep + 1 : beside_all.shape[2] - substep - 1,
        ]
        sample_surfaces = upwind(
            sample_surfaces[:, 1:-1, 1:-1],
            sample_surfaces[:, 1:-1, :-2],
            sample_surfaces[:, 1:-1, 2:],
            sample_surfaces[:, :-2, 1:-1],
            sample_surfaces[:, 2:, 1:-1],
            inner[0],
            inner[1],
            inner[2],
        )
    predicted_sample_vectors = sample_surfaces[:locally_held_samples].astype(jnp.bfloat16)
    prior_mean = sample_surfaces[locally_held_samples]
    total_cells = prior_mean.shape[0] * prior_mean.shape[1]
    cell_table = predicted_sample_vectors.reshape(locally_held_samples, total_cells).T
    tiles = lax.axis_size(LON_LAT)
    block_total = obs_values.shape[0]
    slot_width = obs_values.shape[1]
    capacity = 2 * block_total // tiles
    target = obs_tile[:, 0]
    block_order = jnp.arange(block_total, dtype=jnp.int32)
    same_target = target[:, None] == target[None, :]
    earlier = block_order[:, None] > block_order[None, :]
    position = jnp.sum((same_target & earlier).astype(jnp.int32), 1)
    destination = target * capacity + position
    placement_table = (
        destination[:, None] == jnp.arange(tiles * capacity, dtype=jnp.int32)[None, :]
    ).astype(jnp.float32)
    valid = jnp.arange(slot_width, dtype=jnp.int32)[None, :] < obs_count[:, None]
    weight = jnp.where(valid, 1.0 / obs_variance, 0.0)
    packed = jnp.concatenate([obs_values, weight, obs_cells.astype(jnp.float32)], 1)
    placed = lax.dot_general(
        placement_table, packed, (((0,), (0,)), ((), ())), precision=lax.Precision.HIGHEST
    ).reshape(tiles, capacity, 3, slot_width)
    arrived_values = sent_together(
        (placed[:, :, 0], placed[:, :, 1], placed[:, :, 2]), LON_LAT, 0, 0, 1
    )
    grid_cells = arrived_values[2].reshape(-1).astype(jnp.int32)
    obs_weight = arrived_values[1].reshape(-1)
    obs_misfit = (arrived_values[0].reshape(-1) - prior_mean.reshape(-1)[grid_cells]).astype(
        jnp.bfloat16
    )
    observed = jnp.take(cell_table, grid_cells, axis=0)
    weighted = (observed.astype(jnp.float32) * obs_weight[:, None]).astype(jnp.bfloat16)
    observed_all = lax.all_gather(observed, "mem", axis=1, tiled=True)
    gram_part = lax.dot_general(
        weighted, observed_all, (((0,), (0,)), ((), ())), preferred_element_type=jnp.float32
    )
    projection_part = lax.dot_general(
        weighted, obs_misfit, (((0,), (0,)), ((), ())), preferred_element_type=jnp.float32
    )
    gram_part, projection_part = (
        over_axes(gram_part, LON_LAT),
        over_axes(projection_part, LON_LAT),
    )
    gram, projection = side_by_side((gram_part, projection_part), "mem", 0, 1)
    transform, weights = inverse_root(gram, projection)
    marine_sample_vectors = jnp.concatenate(
        [predicted_sample_vectors[None], delayed_deviation_pair], 0
    )
    flat_states = marine_sample_vectors.reshape(3, locally_held_samples, total_cells)
    first_member = lax.axis_index("mem") * locally_held_samples
    own_columns = lax.dynamic_slice_in_dim(transform, first_member, locally_held_samples, 1)
    segment = lax.all_gather(marine_sample_vectors, "mem", axis=1, tiled=True)
    length = segment.shape[1]
    flat_segment = segment.reshape(3, length, total_cells)
    moved_sum = jnp.einsum(
        "nk,snc->skc", own_columns, flat_segment, preferred_element_type=jnp.float32
    )
    increment_sum = jnp.einsum(
        "n,snc->sc", weights, flat_segment, preferred_element_type=jnp.float32
    )
    wet_flat = wet_mask.reshape(-1)
    states_float = flat_states.astype(jnp.float32)
    blended = (states_float + wet_flat * (moved_sum - states_float)).astype(jnp.bfloat16)
    analysis_anomalies = blended.reshape(marine_sample_vectors.shape)
    state_means = jnp.concatenate([prior_mean[None], lagged_means], 0)
    analysis_mean = state_means + wet_mask * increment_sum.reshape(state_means.shape)
    return (analysis_anomalies, analysis_mean)


def solution(mesh):
    finer = Mesh(
        mesh.devices.reshape(4, 4, mesh.shape["lat"], mesh.shape["mem"]),
        ("lon_0", "lon_1", "lat", "mem"),
    )
    return jax.shard_map(
        body,
        mesh=finer,
        in_specs=(
            P("mem", "lat", LON),
            P("lat", LON),
            P(None, "mem", "lat", LON),
            P(None, "lat", LON),
            P("lat", LON),
            P("lat", LON),
            P("lat", LON),
            P(LON_LAT, None),
            P(LON_LAT, None),
            P(LON_LAT, None),
            P(LON_LAT, None),
            P(LON_LAT),
        ),
        out_specs=(P(None, "mem", "lat", LON), P(None, "lat", LON)),
        check_vma=False,
    )
```

profile of v0, /device:TPU:1, one launch (start us, length us, event | category | flops | bytes accessed | tf_op | source)
XLA Modules:
  0.0 339.2 jit_solution(2044609461510425592)
XLA Ops:
  7.2 1.1 convert_dynamic-update-slice_fusion
  8.3 0.7 bitcast_dynamic-update-slice_fusion.3
  9.0 0.7 bitcast_dynamic-update-slice_fusion.2
  9.8 0.7 bitcast_dynamic-update-slice_fusion.1
  10.5 0.7 bitcast_dynamic-update-slice_fusion
  11.4 0.3 copy.73
  11.7 2.1 collective-permute-start
  13.8 0.3 copy.74
  14.1 3.8 %collective-permute-start.1 = (bf16[68,16,4]{0,1,2:T(8,128)(2,1)S(1)}, bf16[68,16,4]{0,1,2:T(8,128)(2,1)S(1)}, u32[]{:S(2)}, u32[]{:S(2)}) collective-permute-start(bf16[68,16,4]{0,1,2:T(8,128)(2,1)S(1)} %copy.74), channel_id=1, source_target_pairs={{16,0},{32,16},{48,32},{64,48},{80,64},{96,80},{112,96},{128,112},... | collective-permute-start | bytes 26120 | tf_op jit(solution)/shard_map/ppermute | solution.py:22
  18.2 0.4 fusion.57
  19.4 0.6 pad_maximum_fusion.4
  20.0 3.6 %collective-permute-start.2 = (bf16[68,4,264]{2,1,0:T(4,128)(2,1)S(1)}, bf16[68,4,264]{2,1,0:T(4,128)(2,1)S(1)}, u32[]{:S(2)}, u32[]{:S(2)}) collective-permute-start(bf16[68,4,264]{2,1,0:T(4,128)(2,1)S(1)} %get-tuple-element.32), channel_id=1, source_target_pairs={{0,2},{2,4},{4,6},{6,8},{8,10},{10,12},{12,14},{1,3},{3,5},{5,7},{... | collective-permute-start | bytes 430856 | tf_op jit(solution)/shard_map/ppermute | solution.py:21
  23.6 1.3 collective-permute-start.3
  25.4 0.9 reshape.99
  26.3 16.5 %all-to-all-start = ((f32[128,1,384]{2,1,0:T(1,128)}), f32[128,1,384]{2,1,0:T(1,128)S(1)}, u32[]{:S(2)}, u32[]{:S(2)}) async-start(f32[128,1,384]{2,1,0:T(1,128)} %reshape.99), calls=%async_computation | async-start | bytes 393216 | tf_op jit(solution)/shard_map/all_to_all | solution.py:30
  43.7 1.3 maximum_convert_fusion
  44.9 2.6 fusion.28
  47.6 2.6 fusion.19
  50.3 2.6 fusion.10
  53.0 1.2 fusion.50
  54.2 0.7 copy.80
  55.0 2.5 pad_maximum_fusion
  57.8 0.5 broadcast.137
  58.3 1.1 reduce.2
  60.1 57.8 %gather_fusion = bf16[16384,64]{1,0:T(8,128)(2,1)} fusion(bf16[4096,64]{1,0:T(8,128)(2,1)S(1)} %bitcast.187, s32[16384]{0:T(1024)S(1)} %broadcast_clamp_fusion), kind=kCustom, calls=%fused_computation | custom fusion | bytes 4259840 | tf_op jit(solution)/shard_map/jit(_take)/gather | solution.py:154
  118.0 11.6 %broadcast_select_fusion = bf16[16384,64]{1,0:T(8,128)(2,1)} fusion(bf16[16384,64]{1,0:T(8,128)(2,1)} %gather_fusion, pred[16384]{0:T(1024)(128)(4,1)S(1)} %compare_and_fusion), kind=kLoop, calls=%fused_computation.8 | loop fusion | flops 1048576 | bytes 4210688 | tf_op jit(solution)/shard_map/jit(_take)/select_n | solution.py:154
  129.5 4.9 %copy.81 = bf16[16384,64]{0,1:T(8,128)(2,1)} copy(bf16[16384,64]{1,0:T(8,128)(2,1)} %broadcast_select_fusion) | data formatting | bytes 4194304 | tf_op jit(solution)/shard_map/jit(_take)/select_n | solution.py:154
  134.5 1.2 copy-done
  135.7 1.3 concatenate.36
  136.9 0.6 fusion.101
  137.6 0.6 copy.91
  138.2 1.0 concatenate.35
  139.2 0.6 fusion.97
  139.9 90.5 %gather_fusion.1 = f32[16384]{0:T(1024)S(1)} fusion(f32[4096]{0:T(1024)S(1)} %bitcast.186, s32[16384]{0:T(1024)S(1)} %broadcast_clamp_fusion), kind=kCustom, calls=%fused_computation.1 | custom fusion | bytes 196608 | tf_op jit(solution)/shard_map/gather | solution.py:151
  230.7 4.7 %fusion.44 = f32[64]{0:T(128)S(1)} fusion(bf16[16384,1]{0,1:T(2,128)(2,1)S(1)} %reshape.88, bf16[16384,64]{1,0:T(8,128)(2,1)} %broadcast_select_fusion, f32[16384]{0:T(1024)S(1)} %mul.368), kind=kOutput, calls=%fused_computation.72 | convolution fusion | flops 5242880 | bytes 2195712 | tf_op jit(solution)/shard_map/dot_general | solution.py:160
  235.4 4.2 %reshape.65 = bf16[3,128,4096]{2,1,0:T(8,128)(2,1)S(1)} reshape(bf16[3,128,16,256]{3,2,1,0:T(8,128)(2,1)} %all-gather.3.cloned.1.call-done) | data formatting | bytes 6291456 | tf_op jit(solution)/shard_map/reshape | solution.py:177
  239.6 9.7 %fusion.35 = f32[64,128]{1,0:T(8,128)S(1)} fusion(bf16[16384,128]{0,1:T(8,128)(2,1)} %all-gather.5.cloned.1.call-done, bf16[16384,64]{1,0:T(8,128)(2,1)} %broadcast_select_fusion, f32[16384]{0:T(1024)S(1)} %mul.368), kind=kOutput, calls=%fused_computation.52 | convolution fusion | flops 271581184 | bytes 6389760 | tf_op jit(solution)/shard_map/dot_general | solution.py:157
  249.4 13.4 %all-reduce.2 = (f32[64]{0:T(128)S(1)}, f32[64,128]{1,0:T(8,128)S(1)}) all-reduce(f32[64]{0:T(128)S(1)} %fusion.44, f32[64,128]{1,0:T(8,128)S(1)} %fusion.35), channel_id=1, replica_groups=mesh['lon_0'=4,'lon_1'=4,'lat'=8,'mem'=2] {'lon_0'}, use_global_device_ids=true, to_apply=%region_4.5 | all-reduce | flops 8256 | bytes 66048 | tf_op jit(solution)/shard_map/psum | solution.py:36
  262.8 13.7 %all-reduce.1 = (f32[64]{0:T(128)S(1)}, f32[64,128]{1,0:T(8,128)S(1)}) all-reduce(f32[64]{0:T(128)S(1)} %get-tuple-element.6, f32[64,128]{1,0:T(8,128)S(1)} %get-tuple-element.7), channel_id=1, replica_groups=mesh['lon_0'=4,'lon_1'=4,'lat'=8,'mem'=2] {'lon_1'}, use_global_device_ids=true, to_apply=%region_5.6 | all-reduce | flops 8256 | bytes 66048 | tf_op jit(solution)/shard_map/psum | solution.py:36
  276.5 23.1 %all-reduce = (f32[64,1]{1,0:T(8,128)S(1)}, f32[64,128]{1,0:T(8,128)S(1)}) all-reduce(f32[64,1]{1,0:T(8,128)S(1)} %copy.82, f32[64,128]{1,0:T(8,128)S(1)} %get-tuple-element.5), channel_id=1, replica_groups=mesh['lon_0'=4,'lon_1'=4,'lat'=8,'mem'=2] {'lat'}, use_global_device_ids=true, to_apply=%region_6.7 | all-reduce | flops 8256 | bytes 66048 | tf_op jit(solution)/shard_map/psum | solution.py:36
  299.6 19.4 %all_gather.11 = f32[128,129]{1,0:T(8,128)S(1)} all-gather(f32[64,129]{1,0:T(8,128)S(1)} %pad_maximum_fusion.5), channel_id=1, replica_groups=mesh['lon_0'=4,'lon_1'=4,'lat'=8,'mem'=2] {'mem'}, dimensions={0}, use_global_device_ids=true | all-gather | bytes 99072 | tf_op jit(solution)/shard_map/all_gather | solution.py:45
  319.3 0.6 reduce_max.9
  319.9 0.8 fusion.43
  320.7 0.9 fusion.82
  327.2 2.3 fusion.3
  329.6 1.6 copy.93
  331.2 0.5 fusion.4
  331.7 0.6 maximum_add_fusion
  (97 shorter events, 9.2 us)
Async XLA Ops:
  7.2 10.7 %copy-start.5 = (s32[128,64]{0,1:T(8,128)S(1)}, s32[128,64]{0,1:T(8,128)}, u32[]{:S(2)}) copy-start(s32[128,64]{0,1:T(8,128)} %param.21) | copy-start | bytes 98308
  7.2 10.7 %copy-start.10 = (s32[128,1]{0,1:T(1,128)S(1)}, s32[128,1]{0,1:T(1,128)}, u32[]{:S(2)}) copy-start(s32[128,1]{0,1:T(1,128)} %param.22) | copy-start | bytes 1540
  7.2 10.9 %copy-start.6 = (f32[128,64]{0,1:T(8,128)S(1)}, f32[128,64]{0,1:T(8,128)}, u32[]{:S(2)}) copy-start(f32[128,64]{0,1:T(8,128)} %param.20) | copy-start | bytes 98308
  7.2 10.9 %copy-start.9 = (s32[128]{0:T(128)S(1)}, s32[128]{0:T(128)}, u32[]{:S(2)}) copy-start(s32[128]{0:T(128)} %param.23) | copy-start | bytes 1540
  7.2 10.9 %copy-start.7 = (f32[128,64]{0,1:T(8,128)S(1)}, f32[128,64]{0,1:T(8,128)}, u32[]{:S(2)}) copy-start(f32[128,64]{0,1:T(8,128)} %param.19) | copy-start | bytes 98308
  11.7 7.1 %collective-permute-start = (bf16[68,16,4]{0,1,2:T(8,128)(2,1)S(1)}, bf16[68,16,4]{0,1,2:T(8,128)(2,1)S(1)}, u32[]{:S(2)}, u32[]{:S(2)}) collective-permute-start(bf16[68,16,4]{0,1,2:T(8,128)(2,1)S(1)} %copy.73), channel_id=1, source_target_pairs={{0,16},{16,32},{32,48},{48,64},{64,80},{80,96},{96,112},{112,128},... | collective-permute-start | bytes 26120 | tf_op jit(solution)/shard_map/ppermute | solution.py:21
  14.1 5.0 %collective-permute-start.1 = (bf16[68,16,4]{0,1,2:T(8,128)(2,1)S(1)}, bf16[68,16,4]{0,1,2:T(8,128)(2,1)S(1)}, u32[]{:S(2)}, u32[]{:S(2)}) collective-permute-start(bf16[68,16,4]{0,1,2:T(8,128)(2,1)S(1)} %copy.74), channel_id=1, source_target_pairs={{16,0},{32,16},{48,32},{64,48},{80,64},{96,80},{112,96},{128,112},... | collective-permute-start | bytes 26120 | tf_op jit(solution)/shard_map/ppermute | solution.py:22
  20.0 23.1 %collective-permute-start.2 = (bf16[68,4,264]{2,1,0:T(4,128)(2,1)S(1)}, bf16[68,4,264]{2,1,0:T(4,128)(2,1)S(1)}, u32[]{:S(2)}, u32[]{:S(2)}) collective-permute-start(bf16[68,4,264]{2,1,0:T(4,128)(2,1)S(1)} %get-tuple-element.32), channel_id=1, source_target_pairs={{0,2},{2,4},{4,6},{6,8},{8,10},{10,12},{12,14},{1,3},{3,5},{5,7},{... | collective-permute-start | bytes 430856 | tf_op jit(solution)/shard_map/ppermute | solution.py:21
  23.6 19.5 %collective-permute-start.3 = (bf16[68,4,264]{2,1,0:T(4,128)(2,1)S(1)}, bf16[68,4,264]{2,1,0:T(4,128)(2,1)S(1)}, u32[]{:S(2)}, u32[]{:S(2)}) collective-permute-start(bf16[68,4,264]{2,1,0:T(4,128)(2,1)S(1)} %get-tuple-element.33), channel_id=1, source_target_pairs={{2,0},{4,2},{6,4},{8,6},{10,8},{12,10},{14,12},{3,1},{5,3},{7,5},{... | collective-permute-start | bytes 430856 | tf_op jit(solution)/shard_map/ppermute | solution.py:22
  26.3 31.5 %all-to-all-start = ((f32[128,1,384]{2,1,0:T(1,128)}), f32[128,1,384]{2,1,0:T(1,128)S(1)}, u32[]{:S(2)}, u32[]{:S(2)}) async-start(f32[128,1,384]{2,1,0:T(1,128)} %reshape.99), calls=%async_computation | async-start | bytes 393216 | tf_op jit(solution)/shard_map/all_to_all | solution.py:30
  42.8 192.5 %all-gather.3.cloned.1.call-start = ((), (), s32[]{:S(2)}) async-start(), calls=%async_computation.1 | async-start | bytes 4718592 | tf_op jit(solution)/shard_map/all_gather | solution.py:175
  57.5 182.1 %all-gather.5.cloned.1.call-start = ((), (), s32[]{:S(2)}) async-start(), calls=%async_computation.2 | async-start | bytes 6291456 | tf_op jit(solution)/shard_map/all_gather | solution.py:156
  134.4 1.2 copy-start
  134.4 2.5 copy-start.3
  320.7 6.5 %copy-start.8 = (f32[2,2,8,128]{3,1,2,0:T(2,128)S(1)}, f32[2,2,8,128]{3,1,2,0:T(2,128)}, u32[]{:S(2)}) copy-start(f32[2,2,8,128]{3,1,2,0:T(2,128)} %copy.91) | copy-start | bytes 49156
  329.6 2.1 copy-start.1
  329.6 2.1 copy-start.2
  329.6 2.1 copy-start.4
Sparse Core Ops, SparseCore 0:
  57.6 21.3 all-gather.2
  134.6 22.8 all-gather.4
where the time goes:
time: 340 us; the launch traced here: 339 us
  local copies, waits for them, and re-layouts  171 us (50%)
  blocking collectives  69.6 us (20%)
  other arithmetic  31.2 us (9%)
  starting transfers between devices  27.7 us (8%)
  matrix products  24 us (7%)
  between operations  15.4 us (5%)
    gather x1, local copies, waits for them, and re-layouts, body(): prior_mean.reshape(-1)[grid_cells]  90.5 us
    gather x1, local copies, waits for them, and re-layouts, body(): observed = jnp.take(cell_table, grid_cells, axis=0)  57.8 us
    psum x3, blocking collectives, over_axes(): x = lax.psum(x, axis)  50.1 us
    all_gather x1, blocking collectives, side_by_side(): out = lax.all_gather(both, axis, axis=dim, tiled=True)  19.4 us
    all_to_all x1, starting transfers between devices, sent_together(): lax.all_to_all(both, axis, split_axis=split_dim, concat_axis=concat_dim,...  16.5 us
    select_n x2, other arithmetic, body(): observed = jnp.take(cell_table, grid_cells, axis=0)  11.6 us
    dot_general x1, matrix products, body(): lax.dot_general(weighted, observed_all, (((0,), (0,)), ((), ())), preferr...  9.73 us
    sub x4, other arithmetic, upwind(): return center - wet_mask * tendency  8.93 us
  transfers between devices with their start and end apart: 7, of which 0 were waited for; matrix products, arithmetic and copies ran while one was open for 58% of the time, Pallas kernels for 0%

commit v1 on v0

--- a/solution.py
+++ b/solution.py
@@ -33,7 +33,7 @@
 
 def over_axes(x, axes):
     for axis in axes:
-        x = lax.psum(x, axis)
+        x = jnp.sum(lax.all_gather(x, axis), axis=0)
     return x
 
 

time: 340 us -> 366 us (1.076)
  blocking collectives: 69.6 us -> 91.4 us
    psum x3 -> x0, blocking collectives: 50.1 us -> none  [over_axes(): x = lax.psum(x, axis)]
    all_gather x0 -> x3, blocking collectives: none -> 36.7 us  [over_axes(): x = jnp.sum(lax.all_gather(x, axis), axis=0)]
    unnamed x0 -> x3, blocking collectives: none -> 29.9 us
    all_gather x1, blocking collectives: 19.4 us -> 24.8 us  [side_by_side(): out = lax.all_gather(both, axis, axis=dim, tiled=True)]
    unnamed x30 -> x46, local copies, waits for them, and re-layouts: 6.67 us -> 9.26 us
  transfers between devices with their start and end apart: 7 -> 7, of which waited for: 0 -> 0; matrix products, arithmetic and copies ran while one was open for 58% -> 55% of each run, Pallas kernels for 0% -> 0%
where the time goes in v1:
time: 366 us; the launch traced here: 365 us
  local copies, waits for them, and re-layouts  173 us (47%)
  blocking collectives  91.4 us (25%)
  other arithmetic  31.3 us (9%)
  starting transfers between devices  27.7 us (8%)
  matrix products  24 us (7%)
  between operations  17.4 us (5%)
    gather x1, local copies, waits for them, and re-layouts, body(): prior_mean.reshape(-1)[grid_cells]  90.5 us
    gather x1, local copies, waits for them, and re-layouts, body(): observed = jnp.take(cell_table, grid_cells, axis=0)  57.4 us
    all_gather x3, blocking collectives, over_axes(): x = jnp.sum(lax.all_gather(x, axis), axis=0)  36.7 us
    unnamed x3, blocking collectives  29.9 us
    all_gather x1, blocking collectives, side_by_side(): out = lax.all_gather(both, axis, axis=dim, tiled=True)  24.8 us
    all_to_all x1, starting transfers between devices, sent_together(): lax.all_to_all(both, axis, split_axis=split_dim, concat_axis=concat_dim,...  16.5 us
    select_n x2, other arithmetic, body(): observed = jnp.take(cell_table, grid_cells, axis=0)  11.6 us
    dot_general x1, matrix products, body(): lax.dot_general(weighted, observed_all, (((0,), (0,)), ((), ())), preferr...  9.73 us
  transfers between devices with their start and end apart: 7, of which 0 were waited for; matrix products, arithmetic and copies ran while one was open for 55% of the time, Pallas kernels for 0%

profile of v1, /device:TPU:1, one launch (start us, length us, event | category | flops | bytes accessed | tf_op | source)
XLA Modules:
  0.0 365.2 jit_solution(17840899627395616991)
XLA Ops:
  7.2 1.1 convert_dynamic-update-slice_fusion
  8.3 0.7 bitcast_dynamic-update-slice_fusion.3
  9.0 0.7 bitcast_dynamic-update-slice_fusion.2
  9.8 0.7 bitcast_dynamic-update-slice_fusion.1
  10.5 0.7 bitcast_dynamic-update-slice_fusion
  11.7 2.1 collective-permute-start
  14.1 3.8 %collective-permute-start.1 = (bf16[68,16,4]{0,1,2:T(8,128)(2,1)S(1)}, bf16[68,16,4]{0,1,2:T(8,128)(2,1)S(1)}, u32[]{:S(2)}, u32[]{:S(2)}) collective-permute-start(bf16[68,16,4]{0,1,2:T(8,128)(2,1)S(1)} %copy.75), channel_id=1, source_target_pairs={{16,0},{32,16},{48,32},{64,48},{80,64},{96,80},{112,96},{128,112},... | collective-permute-start | bytes 26120 | tf_op jit(solution)/shard_map/ppermute | solution.py:22
  19.4 0.6 pad_maximum_fusion.4
  20.0 3.6 collective-permute-start.2
  23.6 1.3 collective-permute-start.3
  25.4 0.9 reshape.120
  26.3 16.5 %all-to-all-start = ((f32[128,1,384]{2,1,0:T(1,128)}), f32[128,1,384]{2,1,0:T(1,128)S(1)}, u32[]{:S(2)}, u32[]{:S(2)}) async-start(f32[128,1,384]{2,1,0:T(1,128)} %reshape.120), calls=%async_computation | async-start | bytes 393216 | tf_op jit(solution)/shard_map/all_to_all | solution.py:30
  43.7 1.3 maximum_convert_fusion
  44.9 2.6 fusion.28
  47.6 2.6 fusion.19
  50.3 2.6 fusion.10
  53.0 1.2 fusion.50
  54.2 0.7 copy.81
  55.0 2.5 pad_maximum_fusion
  58.3 1.1 reduce.2
  60.1 57.4 %gather_fusion = bf16[16384,64]{1,0:T(8,128)(2,1)} fusion(bf16[4096,64]{1,0:T(8,128)(2,1)S(1)} %bitcast.193, s32[16384]{0:T(1024)S(1)} %broadcast_clamp_fusion), kind=kCustom, calls=%fused_computation | custom fusion | bytes 4259840 | tf_op jit(solution)/shard_map/jit(_take)/gather | solution.py:154
  117.5 11.5 %broadcast_select_fusion = bf16[16384,64]{1,0:T(8,128)(2,1)} fusion(bf16[16384,64]{1,0:T(8,128)(2,1)} %gather_fusion, pred[16384]{0:T(1024)(128)(4,1)S(1)} %compare_and_fusion), kind=kLoop, calls=%fused_computation.8 | loop fusion | flops 1048576 | bytes 4210688 | tf_op jit(solution)/shard_map/jit(_take)/select_n | solution.py:154
  129.0 4.8 %copy.82 = bf16[16384,64]{0,1:T(8,128)(2,1)} copy(bf16[16384,64]{1,0:T(8,128)(2,1)} %broadcast_select_fusion) | data formatting | bytes 4194304 | tf_op jit(solution)/shard_map/jit(_take)/select_n | solution.py:154
  133.8 1.2 copy-done
  135.0 1.3 concatenate.36
  136.9 0.6 dynamic-slice.1
  138.8 0.6 dynamic-slice.2
  140.1 0.6 fusion.101
  140.7 0.6 copy.94
  141.3 1.1 concatenate.35
  142.3 0.6 fusion.97
  143.1 90.5 %gather_fusion.1 = f32[16384]{0:T(1024)S(1)} fusion(f32[4096]{0:T(1024)S(1)} %bitcast.192, s32[16384]{0:T(1024)S(1)} %broadcast_clamp_fusion), kind=kCustom, calls=%fused_computation.1 | custom fusion | bytes 196608 | tf_op jit(solution)/shard_map/gather | solution.py:151
  233.8 4.7 %fusion.44 = f32[64]{0:T(128)S(1)} fusion(bf16[16384,1]{0,1:T(2,128)(2,1)S(1)} %reshape.109, bf16[16384,64]{1,0:T(8,128)(2,1)} %broadcast_select_fusion, f32[16384]{0:T(1024)S(1)} %mul.368), kind=kOutput, calls=%fused_computation.72 | convolution fusion | flops 5242880 | bytes 2195712 | tf_op jit(solution)/shard_map/dot_general | solution.py:160
  238.7 8.3 %all-reduce = f32[256]{0:T(256)S(1)} all-reduce(f32[256]{0:T(256)S(1)} %dynamic-update-slice), channel_id=5, replica_groups=mesh['lon_0'=4,'lon_1'=4,'lat'=8,'mem'=2] {'lon_0'}, use_global_device_ids=true, to_apply=%add | all-reduce | flops 256 | bytes 2048
  247.4 8.5 %all-reduce.1 = f32[256]{0:T(256)S(1)} all-reduce(f32[256]{0:T(256)S(1)} %dynamic-update-slice.1), channel_id=6, replica_groups=mesh['lon_0'=4,'lon_1'=4,'lat'=8,'mem'=2] {'lon_1'}, use_global_device_ids=true, to_apply=%add.1 | all-reduce | flops 256 | bytes 2048
  256.2 13.1 %all-reduce.2 = f32[512]{0:T(512)S(1)} all-reduce(f32[512]{0:T(512)S(1)} %dynamic-update-slice.2), channel_id=7, replica_groups=mesh['lon_0'=4,'lon_1'=4,'lat'=8,'mem'=2] {'lat'}, use_global_device_ids=true, to_apply=%add.2 | all-reduce | flops 512 | bytes 4096
  269.5 4.2 %reshape.65 = bf16[3,128,4096]{2,1,0:T(8,128)(2,1)S(1)} reshape(bf16[3,128,16,256]{3,2,1,0:T(8,128)(2,1)} %all-gather.9.cloned.1.call-done) | data formatting | bytes 6291456 | tf_op jit(solution)/shard_map/reshape | solution.py:177
  273.8 9.7 %fusion.35 = f32[64,128]{1,0:T(8,128)S(1)} fusion(bf16[16384,128]{0,1:T(8,128)(2,1)} %all-gather.11.cloned.1.call-done, bf16[16384,64]{1,0:T(8,128)(2,1)} %broadcast_select_fusion, f32[16384]{0:T(1024)S(1)} %mul.368), kind=kOutput, calls=%fused_computation.52 | convolution fusion | flops 271581184 | bytes 6389760 | tf_op jit(solution)/shard_map/dot_general | solution.py:157
  283.5 9.1 %all-gather = f32[256,128]{1,0:T(8,128)S(1)} all-gather(f32[64,128]{1,0:T(8,128)S(1)} %fusion.35), channel_id=2, replica_groups=mesh['lon_0'=4,'lon_1'=4,'lat'=8,'mem'=2] {'lon_0'}, dimensions={0}, use_global_device_ids=true | all-gather | bytes 163840 | tf_op jit(solution)/shard_map/all_gather | solution.py:36
  292.6 9.2 %all-gather.1 = f32[256,128]{1,0:T(8,128)S(1)} all-gather(f32[64,128]{1,0:T(8,128)S(1)} %reduce_sum.76), channel_id=3, replica_groups=mesh['lon_0'=4,'lon_1'=4,'lat'=8,'mem'=2] {'lon_1'}, dimensions={0}, use_global_device_ids=true | all-gather | bytes 163840 | tf_op jit(solution)/shard_map/all_gather | solution.py:36
  301.8 18.4 %all-gather.2 = f32[512,128]{1,0:T(8,128)S(1)} all-gather(f32[64,128]{1,0:T(8,128)S(1)} %reduce_sum.77), channel_id=4, replica_groups=mesh['lon_0'=4,'lon_1'=4,'lat'=8,'mem'=2] {'lat'}, dimensions={0}, use_global_device_ids=true | all-gather | bytes 294912 | tf_op jit(solution)/shard_map/all_gather | solution.py:36
  320.3 24.8 %all_gather.59 = f32[128,129]{1,0:T(8,128)S(1)} all-gather(f32[64,129]{1,0:T(8,128)S(1)} %pad_maximum_fusion.5), channel_id=1, replica_groups=mesh['lon_0'=4,'lon_1'=4,'lat'=8,'mem'=2] {'mem'}, dimensions={0}, use_global_device_ids=true | all-gather | bytes 99072 | tf_op jit(solution)/shard_map/all_gather | solution.py:45
  345.3 0.6 reduce_max.9
  345.9 0.8 fusion.43
  346.8 0.9 fusion.82
  353.3 2.3 fusion.3
  355.6 1.6 copy.96
  357.8 0.6 maximum_add_fusion
  (124 shorter events, 13.0 us)
Async XLA Ops:
  7.2 10.7 %copy-start.5 = (s32[128,64]{0,1:T(8,128)S(1)}, s32[128,64]{0,1:T(8,128)}, u32[]{:S(2)}) copy-start(s32[128,64]{0,1:T(8,128)} %param.21) | copy-start | bytes 98308
  7.2 10.7 %copy-start.10 = (s32[128,1]{0,1:T(1,128)S(1)}, s32[128,1]{0,1:T(1,128)}, u32[]{:S(2)}) copy-start(s32[128,1]{0,1:T(1,128)} %param.22) | copy-start | bytes 1540
  7.2 10.9 %copy-start.6 = (f32[128,64]{0,1:T(8,128)S(1)}, f32[128,64]{0,1:T(8,128)}, u32[]{:S(2)}) copy-start(f32[128,64]{0,1:T(8,128)} %param.20) | copy-start | bytes 98308
  7.2 10.9 %copy-start.9 = (s32[128]{0:T(128)S(1)}, s32[128]{0:T(128)}, u32[]{:S(2)}) copy-start(s32[128]{0:T(128)} %param.23) | copy-start | bytes 1540
  7.2 10.9 %copy-start.7 = (f32[128,64]{0,1:T(8,128)S(1)}, f32[128,64]{0,1:T(8,128)}, u32[]{:S(2)}) copy-start(f32[128,64]{0,1:T(8,128)} %param.19) | copy-start | bytes 98308
  11.7 7.1 %collective-permute-start = (bf16[68,16,4]{0,1,2:T(8,128)(2,1)S(1)}, bf16[68,16,4]{0,1,2:T(8,128)(2,1)S(1)}, u32[]{:S(2)}, u32[]{:S(2)}) collective-permute-start(bf16[68,16,4]{0,1,2:T(8,128)(2,1)S(1)} %copy.74), channel_id=1, source_target_pairs={{0,16},{16,32},{32,48},{48,64},{64,80},{80,96},{96,112},{112,128},... | collective-permute-start | bytes 26120 | tf_op jit(solution)/shard_map/ppermute | solution.py:21
  14.1 5.0 %collective-permute-start.1 = (bf16[68,16,4]{0,1,2:T(8,128)(2,1)S(1)}, bf16[68,16,4]{0,1,2:T(8,128)(2,1)S(1)}, u32[]{:S(2)}, u32[]{:S(2)}) collective-permute-start(bf16[68,16,4]{0,1,2:T(8,128)(2,1)S(1)} %copy.75), channel_id=1, source_target_pairs={{16,0},{32,16},{48,32},{64,48},{80,64},{96,80},{112,96},{128,112},... | collective-permute-start | bytes 26120 | tf_op jit(solution)/shard_map/ppermute | solution.py:22
  20.0 23.1 %collective-permute-start.2 = (bf16[68,4,264]{2,1,0:T(4,128)(2,1)S(1)}, bf16[68,4,264]{2,1,0:T(4,128)(2,1)S(1)}, u32[]{:S(2)}, u32[]{:S(2)}) collective-permute-start(bf16[68,4,264]{2,1,0:T(4,128)(2,1)S(1)} %get-tuple-element.26), channel_id=1, source_target_pairs={{0,2},{2,4},{4,6},{6,8},{8,10},{10,12},{12,14},{1,3},{3,5},{5,7},{... | collective-permute-start | bytes 430856 | tf_op jit(solution)/shard_map/ppermute | solution.py:21
  23.6 19.5 %collective-permute-start.3 = (bf16[68,4,264]{2,1,0:T(4,128)(2,1)S(1)}, bf16[68,4,264]{2,1,0:T(4,128)(2,1)S(1)}, u32[]{:S(2)}, u32[]{:S(2)}) collective-permute-start(bf16[68,4,264]{2,1,0:T(4,128)(2,1)S(1)} %get-tuple-element.27), channel_id=1, source_target_pairs={{2,0},{4,2},{6,4},{8,6},{10,8},{12,10},{14,12},{3,1},{5,3},{7,5},{... | collective-permute-start | bytes 430856 | tf_op jit(solution)/shard_map/ppermute | solution.py:22
  26.3 31.5 %all-to-all-start = ((f32[128,1,384]{2,1,0:T(1,128)}), f32[128,1,384]{2,1,0:T(1,128)S(1)}, u32[]{:S(2)}, u32[]{:S(2)}) async-start(f32[128,1,384]{2,1,0:T(1,128)} %reshape.120), calls=%async_computation | async-start | bytes 393216 | tf_op jit(solution)/shard_map/all_to_all | solution.py:30
  42.8 226.7 %all-gather.9.cloned.1.call-start = ((), (), s32[]{:S(2)}) async-start(), calls=%async_computation.1 | async-start | bytes 4718592 | tf_op jit(solution)/shard_map/all_gather | solution.py:175
  57.5 216.3 %all-gather.11.cloned.1.call-start = ((), (), s32[]{:S(2)}) async-start(), calls=%async_computation.2 | async-start | bytes 6291456 | tf_op jit(solution)/shard_map/all_gather | solution.py:156
  133.8 1.2 copy-start
  133.8 2.5 copy-start.13
  133.8 3.1 copy-start.12
  133.8 5.0 %copy-start.11 = (u32[256]{0:T(256)S(1)}, u32[256]{0:T(256)}, u32[]{:S(2)}) copy-start(u32[256]{0:T(256)} %constant.61) | copy-start | bytes 3076
  133.8 6.3 %copy-start.3 = (s32[16,256]{1,0:T(8,128)S(1)}, s32[16,256]{1,0:T(8,128)}, u32[]{:S(2)}) copy-start(s32[16,256]{1,0:T(8,128)} %param.18) | copy-start | bytes 49156
  346.8 6.5 %copy-start.8 = (f32[2,2,8,128]{3,1,2,0:T(2,128)S(1)}, f32[2,2,8,128]{3,1,2,0:T(2,128)}, u32[]{:S(2)}) copy-start(f32[2,2,8,128]{3,1,2,0:T(2,128)} %copy.94) | copy-start | bytes 49156
  355.6 2.1 copy-start.1
  355.6 2.1 copy-start.2
  355.6 2.1 copy-start.4
Sparse Core Ops, SparseCore 0:
  57.6 21.3 all-gather.8
  134.0 22.8 all-gather.10
